TPU v7x, 32 devices: a whole 2x2x4 slice. The times are simulated.
32 devices in a mesh: group: 2 (over y), ctx: 4 (over z), head: 2 (over x), dec: 2 (over core).
Axes of the slice: x: 2, y: 2, z: 4, core: 2. Of those that a mesh axis runs over, the one named last changes fastest.
Arguments:
- queries: bfloat16 [1024, 12288], P(('group', 'ctx'), ('head', 'dec')), parts along dimension 0, may hold values from -1100 to 1100
- latent_rows: bfloat16 [1024, 576], P(('group', 'ctx')), parts along dimension 0, may hold values from -8 to 8
- segments: int32 [1024], P('group'), parts along dimension 0, may hold values from 0 to 3, never falling along the last dimension, each value on 1 to 256 neighbouring positions
- owners: int32 [1024, 1], P(('group', 'ctx')), parts along dimension 0, may hold values from 0 to 7; in each aligned block of 128 rows (0 to 127, 128 to 255, ...) at most 32 rows name the same one
- absorb_key: bfloat16 [64, 128, 512], P(('head', 'dec')), may hold values from -0.5 to 0.5
- absorb_value: bfloat16 [64, 512, 128], P(('head', 'dec')), may hold values from -0.25 to 0.25
Outputs:
- attended: bfloat16 [1024, 8192], P(('group', 'ctx'), ('head', 'dec')), parts along dimension 0
- kv_cache: bfloat16 [16, 4, 32, 576], P(('group', 'ctx', 'dec')), parts along dimension 0
There are 2 independent parts, one for each index of `group`. A program takes and returns all parts, laid end to end along the dimension named above; an argument that names none is the same for every part. Nothing has to cross between parts.
Inputs may be any that keep to these rules, and one draw needn't show every extreme that they name: `segments`: prompt numbers never fall along the tokens; each prompt has 1 to 256 tokens and one has exactly 256. `owners`: among the 128 tokens of one index of ctx no owner is named more than 32 times; some owner is named exactly 32 times in some of them; every owner is named somewhere.
All inputs are finite; a program needn't handle non-finite values.
Results may differ from a plain program's by a relative error of at most 0.0085.
Values may be sent and summed in bfloat16 or wider, within the bound.
A program may use at most 128 MiB of HBM per device.

v0:
```python
import jax
import jax.numpy as jnp
from jax import lax
from jax.sharding import PartitionSpec as P

NOPE = 128
ROPE = 64
LATENT = 512
VDIM = 128


def rotate_pairs(rope_part, positions):
    half_rope = ROPE // 2
    frequency = 10000.0 ** (-jnp.arange(half_rope, dtype=jnp.float32) * 2.0 / ROPE)
    angles = positions.astype(jnp.float32)[:, None] * frequency[None, :]
    cosine = jnp.cos(angles)[:, None, :]
    sine_part = jnp.sin(angles)[:, None, :]
    first_part = rope_part[..., :half_rope]
    second = rope_part[..., half_rope:]
    return jnp.concatenate(
        [first_part * cosine - second * sine_part, first_part * sine_part + second * cosine],
        axis=-1,
    )


def ship_rows(latent_rows, owners):
    row_count = latent_rows.shape[0]
    ctx_count = lax.axis_size("ctx")
    dec_count = lax.axis_size("dec")
    core_index = lax.axis_index("dec")
    slots = max(2, 2 * row_count // (ctx_count * dec_count))
    owner_ids = owners[:, 0]
    row_order = jnp.arange(row_count, dtype=jnp.int32)
    earlier = row_order[None, :] < row_order[:, None]
    slot_rank = jnp.sum((owner_ids[:, None] == owner_ids[None, :]) & earlier, axis=1)
    target = owner_ids // dec_count * slots + slot_rank
    kept_rows = owner_ids % dec_count == core_index
    picker = (
        (jnp.arange(ctx_count * slots, dtype=jnp.int32)[:, None] == target[None, :])
        & kept_rows[None, :]
    ).astype(jnp.bfloat16)
    outgoing = jnp.dot(picker, latent_rows, preferred_element_type=jnp.float32).astype(jnp.bfloat16)
    outgoing = outgoing.reshape(ctx_count, slots, LATENT + ROPE)
    arrived = lax.all_to_all(outgoing, "ctx", split_axis=0, concat_axis=0, tiled=True)
    return arrived[None]


def on_device(queries, latent_rows, segments, owners, absorb_key, absorb_value):
    row_count = queries.shape[0]
    local_heads = absorb_key.shape[0]
    width = LATENT + ROPE
    ctx_index = lax.axis_index("ctx")
    scale = (NOPE + ROPE) ** (-0.5)
    shaped = queries.reshape(row_count, local_heads, NOPE + ROPE)
    offsets = jnp.arange(row_count, dtype=jnp.int32)
    query_pos = ctx_index * row_count + offsets
    query_seg = jnp.take(segments, query_pos)
    rotated = rotate_pairs(shaped[..., NOPE:].astype(jnp.float32), query_pos).astype(jnp.bfloat16)
    absorbed = jnp.einsum(
        "thn,hnc->thc", shaped[..., :NOPE], absorb_key, preferred_element_type=jnp.float32
    ).astype(jnp.bfloat16)
    full_query = jnp.concatenate([absorbed, rotated], axis=-1).reshape(
        row_count * local_heads, width
    )
    last_query = jnp.max(query_pos)
    lowest_seg = jnp.min(query_seg)
    highest_seg = jnp.max(query_seg)
    start_state = (
        jnp.full((row_count, local_heads), -1e30, jnp.float32),
        jnp.zeros((row_count, local_heads), jnp.float32),
        jnp.zeros((row_count, local_heads, LATENT), jnp.float32),
    )
    key_piece = lax.all_gather(latent_rows, "ctx", axis=0, tiled=True)
    count = key_piece.shape[0]
    key_pos = jnp.arange(count, dtype=jnp.int32)
    is_live = (
        (jnp.int32(0) <= last_query)
        & (segments[count - 1] >= lowest_seg)
        & (segments[0] <= highest_seg)
    )

    def update(carried):
        running_max, running_sum, running_out = carried
        scores = jnp.einsum("qw,kw->qk", full_query, key_piece, preferred_element_type=jnp.float32)
        scores = scores.reshape(row_count, local_heads, count) * scale
        allowed = (
            (key_pos[None, :] <= query_pos[:, None]) & (segments[None, :] == query_seg[:, None])
        )[:, None, :]
        masked = jnp.where(allowed, scores, -1e30)
        new_max = jnp.maximum(running_max, jnp.max(masked, axis=2))
        weights = jnp.where(allowed, jnp.exp(masked - new_max[..., None]), 0.0)
        new_sum = jnp.sum(weights, axis=2)
        mixed = jnp.dot(
            weights.astype(jnp.bfloat16).reshape(row_count * local_heads, count),
            key_piece[:, :LATENT],
            preferred_element_type=jnp.float32,
        )
        new_out = mixed.reshape(row_count, local_heads, LATENT)
        return (new_max, new_sum, new_out)

    final_state = lax.cond(is_live, update, lambda carried: carried, start_state)
    running_max, running_sum, running_out = final_state
    latent_out = (running_out / running_sum[..., None]).astype(jnp.bfloat16)
    answer = jnp.einsum(
        "thc,hcv->thv", latent_out, absorb_value, preferred_element_type=jnp.float32
    ).astype(jnp.bfloat16)
    answer = answer.reshape(row_count, local_heads * VDIM)
    kv_cache = ship_rows(latent_rows, owners)
    return (answer, kv_cache)


def solution(mesh):
    in_specs = (
        P(("group", "ctx"), ("head", "dec")),
        P(("group", "ctx"), None),
        P("group"),
        P(("group", "ctx"), None),
        P(("head", "dec"), None, None),
        P(("head", "dec"), None, None),
    )
    out_specs = (P(("group", "ctx"), ("head", "dec")), P(("group", "ctx", "dec"), None, None, None))
    return jax.shard_map(
        on_device, mesh=mesh, in_specs=in_specs, out_specs=out_specs, check_vma=False
    )
```

profile of v0, /device:TPU:0, one launch (start us, length us, event | category | flops | bytes accessed | tf_op | source)
XLA Modules:
  0.0 66.6 jit_solution(2304539550572931072)
XLA Ops:
  0.6 0.0 copy-start
  0.6 0.0 copy-start.1
  0.7 0.8 %fusion.15 = pred[128]{0:T(512)(128)(4,1)S(1)} fusion(s32[]{:T(128)S(6)} %axis_index.25, s32[128,1]{0,1:T(1,128)} %param.11), kind=kLoop, calls=%fused_computation.40 | loop fusion | flops 1536 | bytes 644 | tf_op jit(solution)/shard_map/eq | solution.py:37
  1.5 0.9 %convert_reduce_fusion = s32[128]{0:T(128)S(1)} fusion(s32[128]{0:T(128)} %bitcast.45), kind=kLoop, calls=%fused_computation.22 | loop fusion | flops 81792 | bytes 1024 | tf_op jit(solution)/shard_map/reduce_sum | solution.py:35
  2.4 0.7 %multiply_add_fusion = s32[128]{0:T(128)S(1)} fusion(s32[128]{0:T(128)S(1)} %convert_reduce_fusion, s32[128,1]{0,1:T(1,128)} %param.11), kind=kLoop, calls=%fused_computation.42 | loop fusion | flops 2176 | bytes 1536 | tf_op jit(solution)/shard_map/add | solution.py:36
  3.1 1.1 %convolution_convert_fusion = bf16[128,576]{0,1:T(8,128)(2,1)S(1)} fusion(bf16[128,576]{0,1:T(8,128)(2,1)} %param.9, s32[128]{0:T(128)S(1)} %multiply_add_fusion, pred[128]{0:T(512)(128)(4,1)S(1)} %fusion.15), kind=kOutput, calls=%fused_computation.17 | convolution fusion | flops 18980864 | bytes 295552 | tf_op jit(solution)/shard_map/dot_general | solution.py:42
  4.2 0.8 %copy.36 = bf16[128,576]{1,0:T(8,128)(2,1)} copy(bf16[128,576]{0,1:T(8,128)(2,1)S(1)} %convolution_convert_fusion) | data formatting | bytes 294912 | tf_op jit(solution)/shard_map/convert_element_type | solution.py:42
  5.0 6.3 %all-to-all-start = ((bf16[4,32,576]{2,1,0:T(8,128)(2,1)}), bf16[4,32,576]{2,1,0:T(8,128)(2,1)}, u32[]{:S(2)}, u32[]{:S(2)}) async-start(bf16[4,32,576]{2,1,0:T(8,128)(2,1)} %bitcast.12), calls=%async_computation | async-start | bytes 327680 | tf_op jit(solution)/shard_map/all_to_all | solution.py:44
  11.3 0.6 fusion.17
  12.0 1.7 %copy.32 = bf16[128,576]{1,0:T(8,128)(2,1)} copy(bf16[128,576]{0,1:T(8,128)(2,1)} %param.9) | data formatting | bytes 294912 | tf_op args[1]
  13.7 1.5 %copy.29 = bf16[128,3072]{0,1:T(8,128)(2,1)S(1)} copy(bf16[128,3072]{1,0:T(8,128)(2,1)} %param.8) | data formatting | bytes 1572864 | tf_op args[0]
  15.3 0.0 copy-done
  15.3 2.1 %convert_bitcast_fusion = bf16[128,16,512]{0,2,1:T(8,128)(2,1)} fusion(bf16[16,128,512]{2,1,0:T(8,128)(2,1)S(1)} %copy-done, bf16[128,16,192]{0,2,1:T(8,128)(2,1)S(1)} %bitcast.43), kind=kOutput, calls=%fused_computation.14 | convolution fusion | flops 269484032 | bytes 4718592 | tf_op jit(solution)/shard_map/thn,hnc->thc/dot_general | solution.py:59
  17.4 0.0 copy-done.1
  17.4 0.6 fusion.20
  18.0 1.3 %gather_fusion = s32[128]{0:T(128)S(1)} fusion(s32[512]{0:T(512)S(1)} %copy-done.1, s32[1024]{0:T(1024)S(1)} %pad_clamp_fusion), kind=kCustom, calls=%fused_computation | custom fusion | bytes 1536 | tf_op jit(solution)/shard_map/jit(_take)/gather | solution.py:57
  19.3 0.6 fusion.19
  19.9 18.1 %all_gather.3 = bf16[512,576]{1,0:T(8,128)(2,1)S(1)} all-gather(bf16[128,576]{1,0:T(8,128)(2,1)} %copy.32), channel_id=1, replica_groups=mesh['group'=2,'ctx'=4,'head'=2,'dec'=2] {'ctx'}, dimensions={0}, use_global_device_ids=true | all-gather | bytes 737280 | tf_op jit(solution)/shard_map/all_gather | solution.py:73
  41.1 0.1 multiply_cosine_fusion
  41.2 0.1 subtract_convert_fusion
  41.3 3.2 %pad_maximum_fusion = bf16[128,16,576]{0,2,1:T(8,128)(2,1)} fusion(bf16[128,16,32]{0,2,1:T(8,128)(2,1)S(1)} %get-tuple-element.57, bf16[128,16,32]{0,2,1:T(8,128)(2,1)S(1)} %get-tuple-element.56, bf16[128,16,512]{0,2,1:T(8,128)(2,1)} %convert_bitcast_fusion), kind=kLoop, calls=%fused_computation.13 | loop fusion | flops 7077888 | bytes 4718592 | tf_op jit(solution)/shard_map/concatenate | solution.py:62
  44.5 15.3 %conditional.1 = (f32[128,16]{1,0:T(8,128)S(1)}, f32[128,16,512]{2,0,1:T(8,128)}) conditional(s32[]{:T(128)} %convert_element_type.40, () %tuple.16, (s32[512]{0:T(512)S(1)}, s32[128]{0:T(128)S(1)}, s32[512]{0:T(512)S(1)}, s32[128]{0:T(128)S(1)}, bf16[128,16,576]{0,2,1:T(8,128)(2,1)}, /*index=5*/bf16[512,576]{1,0:T(8,128)(2,1)S(1)}) %tuple.38), branch_computations={%region_3.4_spmd, %region_4.0_spmd} | conditional | flops 2291333120 | bytes 25228304 | solution.py:101
  44.5 0.1 compare_and_fusion
  44.7 4.9 %copy.33 = bf16[128,16,576]{2,1,0:T(8,128)(2,1)} copy(bf16[128,16,576]{0,2,1:T(8,128)(2,1)} %get-tuple-element.45) | data formatting | bytes 4718592 | tf_op jit(solution)/shard_map
  49.6 4.0 %fusion = (f32[2048]{0:T(1024)S(1)}, f32[2048,512]{1,0:T(8,128)S(1)}) fusion(pred[128,512]{1,0:T(8,128)(4,1)S(1)} %compare_and_fusion, bf16[2048,576]{1,0:T(8,128)(2,1)} %bitcast.40, bf16[512,576]{1,0:T(8,128)(2,1)S(1)} %get-tuple-element.18), kind=kOutput, calls=%fused_computation.3 | convolution fusion | flops 1211103232 | bytes 7217152 | tf_op jit(solution)/shard_map/cond/branch_1_fun/qw,kw->qk/dot_general | solution.py:84
  53.6 1.7 %fusion.1 = (bf16[2048,512]{1,0:T(8,128)(2,1)S(1)}, f32[2048]{0:T(1024)S(1)}) fusion(f32[2048,512]{1,0:T(8,128)S(1)} %get-tuple-element.55, f32[2048]{0:T(1024)S(1)} %broadcast_maximum_fusion, pred[128,512]{1,0:T(8,128)(4,1)S(1)} %compare_and_fusion), kind=kLoop, calls=%fused_computation.4 | loop fusion | flops 6289408 | bytes 6373376 | tf_op jit(solution)/shard_map/cond/branch_1_fun/convert_element_type | solution.py:94
  55.3 4.5 %fusion.3 = f32[128,16,512]{2,0,1:T(8,128)} fusion(bf16[128,16,512]{2,1,0:T(8,128)(2,1)S(1)} %bitcast.41, bf16[512,576]{1,0:T(8,128)(2,1)S(1)} %get-tuple-element.18), kind=kOutput, calls=%fused_computation.6 | convolution fusion | flops 1073741824 | bytes 6815744 | tf_op jit(solution)/shard_map/cond/branch_1_fun/dot_general | solution.py:93
  59.8 0.1 reduce_sum.18
  59.9 0.1 copy.34
  59.9 4.0 %fusion.8 = bf16[16,128,128]{1,2,0:T(8,128)(2,1)S(1)} fusion(bf16[16,512,128]{2,1,0:T(8,128)(2,1)} %param.13, f32[128,16,512]{2,0,1:T(8,128)} %get-tuple-element.23, f32[128,16]{0,1:T(8,128)S(1)} %copy.34), kind=kOutput, calls=%fused_computation.16 | convolution fusion | flops 270794752 | bytes 6823936 | tf_op jit(solution)/shard_map/thc,hcv->thv/dot_general | solution.py:104
  63.9 1.0 %copy.37 = bf16[128,2048]{1,0:T(8,128)(2,1)} copy(bf16[128,2048]{0,1:T(8,128)(2,1)S(1)} %bitcast.44) | data formatting | bytes 1048576
  65.0 0.0 all-to-all-done
  65.0 1.6 %copy.48 = bf16[1,4,32,576]{3,2,1,0:T(8,128)(2,1)} copy(bf16[1,4,32,576]{3,2,1,0:T(8,128)(2,1)} %bitcast.13) | data formatting | bytes 294912
  (6 shorter events, 0.1 us)
Async XLA Ops:
  0.6 14.6 %copy-start = (bf16[16,128,512]{2,1,0:T(8,128)(2,1)S(1)}, bf16[16,128,512]{2,1,0:T(8,128)(2,1)}, u32[]{:S(2)}) copy-start(bf16[16,128,512]{2,1,0:T(8,128)(2,1)} %param.12) | copy-start | bytes 6291460
  0.6 16.8 %copy-start.1 = (s32[512]{0:T(512)S(1)}, s32[512]{0:T(512)}, u32[]{:S(2)}) copy-start(s32[512]{0:T(512)} %param.10) | copy-start | bytes 6148
  5.0 60.0 %all-to-all-start = ((bf16[4,32,576]{2,1,0:T(8,128)(2,1)}), bf16[4,32,576]{2,1,0:T(8,128)(2,1)}, u32[]{:S(2)}, u32[]{:S(2)}) async-start(bf16[4,32,576]{2,1,0:T(8,128)(2,1)} %bitcast.12), calls=%async_computation | async-start | bytes 327680 | tf_op jit(solution)/shard_map/all_to_all | solution.py:44
where the time goes:
time: 67.1 us; the launch traced here: 66.6 us
  blocking collectives  18.1 us (27%)
  matrix products  15.7 us (23%)
  local copies, waits for them, and re-layouts  13.6 us (20%)
  other arithmetic  8.98 us (13%)
  starting transfers between devices  6.35 us (9%)
  between operations  3.79 us (6%)
    all_gather x1, blocking collectives, on_device(): key_piece = lax.all_gather(latent_rows, 'ctx', axis=0, tiled=True)  18.1 us
    all_to_all x1, starting transfers between devices, ship_rows(): lax.all_to_all(outgoing, 'ctx', split_axis=0, concat_axis=0, tiled=True)  6.35 us
    unnamed x8, local copies, waits for them, and re-layouts  5.85 us
    another operation x1, local copies, waits for them, and re-layouts  4.93 us
    dot_general x1, matrix products, update(): jnp.dot(weights.astype(jnp.bfloat16).reshape(row_count * local_heads, cou...  4.52 us
    dot_general x1, matrix products, update(): jnp.einsum('qw,kw->qk', full_query, key_piece, preferred_element_type=jnp...  3.99 us
    dot_general x1, matrix products, on_device(): jnp.einsum('thc,hcv->thv', latent_out, absorb_value, preferred_element_ty...  3.98 us
    concatenate x1, other arithmetic, on_device(): jnp.concatenate([absorbed, rotated], axis=-1)  3.23 us
  transfers between devices with their start and end apart: 1, of which 0 were waited for; matrix products, arithmetic and copies ran while one was open for 49% of the time, Pallas kernels for 0%

commit v1 on v0

v1 whole, which is shorter than its diff:
```python
import functools

import jax
import jax.numpy as jnp
from jax import lax
from jax.experimental import pallas as pl
from jax.experimental.pallas import tpu as pltpu
from jax.sharding import PartitionSpec as P

NOPE = 128
ROPE = 64
LATENT = 512
VDIM = 128
MESH = pl.DeviceIdType.MESH
NEG = -1e30


def cdiv(a, b):
    return -(-a // b)


def kernel(
    n, cores, back, slots, chunk,
    freq_ref, seg_ref, owners_hbm, rows_hbm, q_hbm, ak_hbm, av_hbm,
    out_ref, kv_ref,
    qv, ak, av, qf, acc, m_ref, l_ref, held, owners,
    local_sem, send_sem, recv_sem, fsend_sem, frecv_sem, osend_sem, orecv_sem,
):
    c = lax.axis_index("ctx")
    d = lax.axis_index("dec")
    rows = rows_hbm.shape[0]
    heads = ak_hbm.shape[0]
    part = rows // cores
    scale = (NOPE + ROPE) ** (-0.5)
    last = n - 1

    loads = [
        pltpu.make_async_copy(rows_hbm, held.at[last], local_sem.at[0]),
        pltpu.make_async_copy(q_hbm, qv, local_sem.at[1]),
        pltpu.make_async_copy(ak_hbm, ak, local_sem.at[2]),
        pltpu.make_async_copy(av_hbm, av, local_sem.at[3]),
        pltpu.make_async_copy(owners_hbm, owners.at[last], local_sem.at[4]),
    ]
    for load in loads:
        load.start()

    barrier = pltpu.get_barrier_semaphore()
    for j in range(1, n):
        pl.semaphore_signal(
            barrier, inc=1, device_id={"ctx": lax.rem(c + j, n)}, device_id_type=MESH
        )
    for k in range(1, cores):
        pl.semaphore_signal(
            barrier, inc=1, device_id={"dec": lax.rem(d + k, cores)}, device_id_type=MESH
        )
    pl.semaphore_wait(barrier, n - 1 + cores - 1)

    mine = pl.ds(pl.multiple_of(d * part, part), part)
    sends = {}
    for j in range(1, n):
        target = {"ctx": lax.rem(c + j, n)}
        sends[j] = pltpu.make_async_remote_copy(
            src_ref=rows_hbm.at[mine],
            dst_ref=held.at[last - j, mine],
            send_sem=send_sem.at[j],
            recv_sem=recv_sem.at[j],
            device_id=target,
            device_id_type=MESH,
        )
        sends[j].start()
    osends = []
    for j in range(1, n):
        copy = pltpu.make_async_remote_copy(
            src_ref=owners_hbm,
            dst_ref=owners.at[last - j],
            send_sem=osend_sem.at[j],
            recv_sem=orecv_sem.at[j],
            device_id={"ctx": lax.rem(c + j, n)},
            device_id_type=MESH,
        )
        copy.start()
        osends.append(copy)

    forwards = {}

    def forward(j):
        sends[j].wait_recv()
        for k in range(1, cores):
            copy = pltpu.make_async_remote_copy(
                src_ref=held.at[last - j, mine],
                dst_ref=held.at[last - j, mine],
                send_sem=fsend_sem.at[j, k],
                recv_sem=frecv_sem.at[j, k],
                device_id={"dec": lax.rem(d + k, cores)},
                device_id_type=MESH,
            )
            copy.start()
            forwards[j, k] = copy

    lane = lax.broadcasted_iota(jnp.int32, (rows, 2 * ROPE), 1) % ROPE
    position = (lax.broadcasted_iota(jnp.int32, (rows, 2 * ROPE), 0) + c * rows).astype(jnp.float32)
    angles = position * freq_ref[0:1, :]
    low = lane < ROPE // 2
    cosine = jnp.cos(angles)
    sine = jnp.sin(angles)
    sine = jnp.where(low, -sine, sine)

    seg_now = seg_ref[pl.ds(c, 1), :].astype(jnp.float32)
    query_seg = jnp.transpose(jnp.broadcast_to(seg_now, (rows, rows)))
    row_id = lax.broadcasted_iota(jnp.int32, (rows, rows), 0)
    col_id = lax.broadcasted_iota(jnp.int32, (rows, rows), 1)

    def mask_of(j):
        key_seg = seg_ref[pl.ds(lax.rem(c - j + n, n), 1), :].astype(jnp.float32)
        same = query_seg == jnp.broadcast_to(key_seg, (rows, rows))
        if j == 0:
            return same & (col_id <= row_id)
        valid = jnp.broadcast_to(c, (rows, rows)) >= j
        return same & valid

    loads[1].wait()
    loads[2].wait()
    pair_width = 2 * (NOPE + ROPE)

    @pl.loop(0, heads // 2)
    def _(p):
        qp = qv[:, pl.ds(pl.multiple_of(p * pair_width, 128), pair_width)]
        rope = jnp.concatenate(
            [qp[:, NOPE:NOPE + ROPE], qp[:, 2 * NOPE + ROPE:]], axis=1
        ).astype(jnp.float32)
        swapped = jnp.where(
            low,
            pltpu.roll(rope, 2 * ROPE - ROPE // 2, 1),
            pltpu.roll(rope, ROPE // 2, 1),
        )
        rotated = (rope * cosine + swapped * sine).astype(jnp.bfloat16)
        qf[2 * p, :, LATENT:] = rotated[:, :ROPE]
        qf[2 * p + 1, :, LATENT:] = rotated[:, ROPE:]
        for k, start in ((0, 0), (1, NOPE + ROPE)):
            qf[2 * p + k, :, :LATENT] = jnp.dot(
                qp[:, start:start + NOPE], ak[2 * p + k], preferred_element_type=jnp.float32
            ).astype(jnp.bfloat16)

    if n > 1:
        forward(1)
    loads[0].wait()
    size = chunk * rows
    own_mask = mask_of(0)

    def scores_of(i, keys, mask):
        q = qf[pl.ds(i * chunk, chunk)].reshape(size, LATENT + ROPE)
        s = lax.dot_general(
            q, keys, (((1,), (1,)), ((), ())), preferred_element_type=jnp.float32
        )
        s = s.reshape(chunk, rows, keys.shape[0]) * scale
        return jnp.where(mask[None], s, NEG).reshape(size, keys.shape[0])

    def finish(i, total, sums):
        latent = (total / sums).astype(jnp.bfloat16)
        for k in range(chunk):
            h = i * chunk + k
            out_ref[:, pl.ds(pl.multiple_of(h * VDIM, VDIM), VDIM)] = jnp.dot(
                latent[k * rows:(k + 1) * rows], av[h], preferred_element_type=jnp.float32
            ).astype(jnp.bfloat16)

    @pl.loop(0, heads // chunk)
    def _(i):
        keys = held[last]
        s = scores_of(i, keys, own_mask)
        top = jnp.max(s, axis=1, keepdims=True)
        e = jnp.exp(s - top)
        at = pl.ds(pl.multiple_of(i * size, size), size)
        m_ref[at] = top
        l_ref[at] = jnp.sum(e, axis=1, keepdims=True)
        acc[at] = jnp.dot(
            e.astype(jnp.bfloat16), keys[:, :LATENT], preferred_element_type=jnp.float32
        )

    groups = [list(range(j, min(j + 2, back + 1))) for j in range(1, back + 1, 2)]
    waited = set()

    def settle(j):
        for k in range(1, cores):
            forwards[j, k].wait_recv()
        waited.add(j)

    loads[3].wait()
    for g, group in enumerate(groups):
        for j in group:
            if j > 1:
                forward(j)
        for j in group:
            settle(j)
        mask = jnp.concatenate([mask_of(j) for j in reversed(group)], axis=1)
        lo, hi = last - group[-1], last - group[0] + 1
        final = g == len(groups) - 1

        def step(i):
            keys = held[lo:hi].reshape((hi - lo) * rows, LATENT + ROPE)
            s = scores_of(i, keys, mask)
            at = pl.ds(pl.multiple_of(i * size, size), size)
            before = m_ref[at]
            top = jnp.maximum(before, jnp.max(s, axis=1, keepdims=True))
            e = jnp.exp(s - top)
            shrink = jnp.exp(before - top)
            sums = l_ref[at] * shrink + jnp.sum(e, axis=1, keepdims=True)
            total = acc[at] * shrink + jnp.dot(
                e.astype(jnp.bfloat16), keys[:, :LATENT], preferred_element_type=jnp.float32
            )
            if final:
                finish(i, total, sums)
            else:
                m_ref[at] = top
                l_ref[at] = sums
                acc[at] = total

        middle = (heads // chunk) // 2 if final else heads // chunk
        pl.loop(0, middle)(step)
        if final:
            for j in range(back + 1, n):
                forward(j)
            pl.loop(middle, heads // chunk)(step)

    for j in range(1, n):
        if j not in waited:
            settle(j)
    loads[4].wait()
    for copy in osends:
        copy.wait()

    me = c * cores + d
    before_tri = (row_id < col_id).astype(jnp.bfloat16)
    slot_id = lax.broadcasted_iota(jnp.int32, (slots, rows), 0).astype(jnp.float32)
    for j in range(n):
        named = owners[last - j, 0:8] == me
        rank = jnp.dot(
            named.astype(jnp.bfloat16), before_tri, preferred_element_type=jnp.float32
        )
        rank = jnp.where(named, rank, -1.0)
        picker = (jnp.broadcast_to(rank[0:1], (slots, rows)) == slot_id).astype(jnp.bfloat16)
        kv_ref[0, lax.rem(c - j + n, n)] = jnp.dot(
            picker, held[last - j], preferred_element_type=jnp.float32
        ).astype(jnp.bfloat16)

    for j in range(1, n):
        sends[j].wait_send()
        for k in range(1, cores):
            forwards[j, k].wait_send()


def on_device(sizes, queries, latent_rows, segments, owners, absorb_key, absorb_value):
    n, cores = sizes
    rows = latent_rows.shape[0]
    width = LATENT + ROPE
    heads = absorb_key.shape[0]
    tokens = segments.shape[0]
    back = min(n - 1, cdiv(tokens // 2 - 1, rows))
    slots = max(2, 2 * rows // (n * cores))
    chunk = 4
    frequency = 10000.0 ** (-jnp.arange(ROPE // 2, dtype=jnp.float32) * 2.0 / ROPE)
    frequency = jnp.broadcast_to(jnp.tile(frequency, 4)[None, :], (8, 2 * ROPE))
    segment_rows = segments.reshape(n, rows)
    owner_rows = jnp.broadcast_to(owners.reshape(1, rows), (8, rows))
    vmem = pl.BlockSpec(memory_space=pltpu.VMEM)
    hbm = pl.BlockSpec(memory_space=pl.ANY)
    dma = pltpu.SemaphoreType.DMA
    return tuple(pl.pallas_call(
        functools.partial(kernel, n, cores, back, slots, chunk),
        out_shape=(
            jax.ShapeDtypeStruct((rows, heads * VDIM), jnp.bfloat16),
            jax.ShapeDtypeStruct((1, n, slots, width), jnp.bfloat16),
        ),
        in_specs=[vmem, vmem, hbm, hbm, hbm, hbm, hbm],
        out_specs=(vmem, vmem),
        scratch_shapes=[
            pltpu.VMEM(queries.shape, jnp.bfloat16),
            pltpu.VMEM(absorb_key.shape, jnp.bfloat16),
            pltpu.VMEM(absorb_value.shape, jnp.bfloat16),
            pltpu.VMEM((heads, rows, width), jnp.bfloat16),
            pltpu.VMEM((heads * rows, LATENT), jnp.float32),
            pltpu.VMEM((heads * rows, 1), jnp.float32),
            pltpu.VMEM((heads * rows, 1), jnp.float32),
            pltpu.VMEM((n, rows, width), jnp.bfloat16),
            pltpu.VMEM((n, 8, rows), jnp.int32),
            dma((5,)),
            dma((n,)),
            dma((n,)),
            dma((n, cores)),
            dma((n, cores)),
            dma((n,)),
            dma((n,)),
        ],
        compiler_params=pltpu.CompilerParams(
            collective_id=0, has_side_effects=True, vmem_limit_bytes=48 * 1024 * 1024
        ),
    )(frequency, segment_rows, owner_rows, latent_rows, queries, absorb_key, absorb_value))


def solution(mesh):
    in_specs = (
        P(("group", "ctx"), ("head", "dec")),
        P(("group", "ctx"), None),
        P("group"),
        P(("group", "ctx"), None),
        P(("head", "dec"), None, None),
        P(("head", "dec"), None, None),
    )
    out_specs = (P(("group", "ctx"), ("head", "dec")), P(("group", "ctx", "dec"), None, None, None))
    sizes = (mesh.shape["ctx"], mesh.shape["dec"])
    return jax.shard_map(
        functools.partial(on_device, sizes),
        mesh=mesh, in_specs=in_specs, out_specs=out_specs, check_vma=False,
    )
```

time: 67.1 us -> 32.2 us (0.48)
  the two profiles are of different devices: /device:TPU:0 before, /device:TPU:21 now
where the time goes in v1:
time: 32.2 us; the launch traced here: 31.9 us
  Pallas kernels  23 us (71%)
  local copies, waits for them, and re-layouts  8.26 us (26%)
  between operations  0.66 us (2%)
    pallas_call x1, Pallas kernels, on_device(): pl.pallas_call(functools.partial(kernel, n, cores, back, slots, chunk), o...  23 us
    unnamed x11, local copies, waits for them, and re-layouts  7.51 us
    broadcast_in_dim x1, local copies, waits for them, and re-layouts, on_device(): owner_rows = jnp.broadcast_to(owners.reshape(1, rows), (8, rows))  0.66 us

profile of v1, /device:TPU:21, one launch (start us, length us, event | category | flops | bytes accessed | tf_op | source)
XLA Modules:
  0.0 31.9 jit_solution(252920314851515401)
XLA Ops:
  0.7 0.1 broadcast_in_dim.14
  0.7 0.7 %broadcast_in_dim.17.owners_hbm = s32[8,128]{1,0:T(8,128)S(1)} broadcast(s32[128]{0:T(128)} %bitcast.3), dimensions={1} | broadcast | bytes 4608 | tf_op jit(solution)/shard_map/broadcast_in_dim | solution.py:263
  1.4 1.1 %copy.8.rows_hbm = bf16[128,576]{1,0:T(8,128)(2,1)S(1)} copy(bf16[128,576]{0,1:T(8,128)(2,1)} %param.7) | data formatting | bytes 294912 | tf_op args[1]
  2.5 0.0 copy-start
  2.5 1.6 %copy-done = bf16[16,128,512]{2,1,0:T(8,128)(2,1)S(1)} copy-done((bf16[16,128,512]{2,1,0:T(8,128)(2,1)S(1)}, bf16[16,128,512]{2,1,0:T(8,128)(2,1)}, u32[]{:S(2)}) %copy-start) | copy-done | bytes 2097176
  4.1 0.0 copy-start.1
  4.1 1.6 %copy-done.1 = bf16[16,512,128]{2,1,0:T(8,128)(2,1)S(1)} copy-done((bf16[16,512,128]{2,1,0:T(8,128)(2,1)S(1)}, bf16[16,512,128]{2,1,0:T(8,128)(2,1)}, u32[]{:S(2)}) %copy-start.1) | copy-done | bytes 2097176
  5.6 0.0 copy-start.2
  5.7 1.1 %copy-done.2 = bf16[128,3072]{1,0:T(8,128)(2,1)S(1)} copy-done((bf16[128,3072]{1,0:T(8,128)(2,1)S(1)}, bf16[128,3072]{1,0:T(8,128)(2,1)}, u32[]{:S(2)}) %copy-start.2) | copy-done | bytes 786456
  6.8 0.0 copy-start.3
  6.8 0.7 %copy-done.3 = s32[512]{0:T(512)S(1)} copy-done((s32[512]{0:T(512)S(1)}, s32[512]{0:T(512)}, u32[]{:S(2)}) %copy-start.3) | copy-done | bytes 2072
  7.5 23.0 %shard_map.77 = (bf16[128,2048]{1,0:T(8,128)(2,1)S(1)}, bf16[1,4,32,576]{3,2,1,0:T(8,128)(2,1)S(1)}) custom-call(f32[8,128]{1,0:T(8,128)S(1)} %broadcast_in_dim.15.freq_ref, s32[4,128]{1,0:T(4,128)S(1)} %bitcast.2, s32[8,128]{1,0:T(8,128)S(1)} %broadcast_in_dim.17.owners_hbm, bf16[128,576]{1,0:T(8,128)(2,1)S(1)} %copy.8.rows_hbm, ...), custom_call_target="tpu_custom_call" | custom-call | tf_op jit(solution)/shard_map/pallas_call | solution.py:267
  30.4 0.8 %copy.11 = bf16[128,2048]{1,0:T(8,128)(2,1)} copy(bf16[128,2048]{1,0:T(8,128)(2,1)S(1)} %get-tuple-element.4) | data formatting | bytes 1048576
  31.2 0.7 %copy.12 = bf16[1,4,32,576]{3,2,1,0:T(8,128)(2,1)} copy(bf16[1,4,32,576]{3,2,1,0:T(8,128)(2,1)S(1)} %get-tuple-element.5) | data formatting | bytes 294912
  (3 shorter events, 0.0 us)
Async XLA Ops:
  2.5 1.6 %copy-start = (bf16[16,128,512]{2,1,0:T(8,128)(2,1)S(1)}, bf16[16,128,512]{2,1,0:T(8,128)(2,1)}, u32[]{:S(2)}) copy-start(bf16[16,128,512]{2,1,0:T(8,128)(2,1)} %ak_hbm.1) | copy-start | bytes 6291460
  4.1 1.6 %copy-start.1 = (bf16[16,512,128]{2,1,0:T(8,128)(2,1)S(1)}, bf16[16,512,128]{2,1,0:T(8,128)(2,1)}, u32[]{:S(2)}) copy-start(bf16[16,512,128]{2,1,0:T(8,128)(2,1)} %av_hbm.1) | copy-start | bytes 6291460
  5.6 1.1 %copy-start.2 = (bf16[128,3072]{1,0:T(8,128)(2,1)S(1)}, bf16[128,3072]{1,0:T(8,128)(2,1)}, u32[]{:S(2)}) copy-start(bf16[128,3072]{1,0:T(8,128)(2,1)} %q_hbm.1) | copy-start | bytes 2359300
  6.8 0.7 %copy-start.3 = (s32[512]{0:T(512)S(1)}, s32[512]{0:T(512)}, u32[]{:S(2)}) copy-start(s32[512]{0:T(512)} %param.8) | copy-start | bytes 6148

commit v2 on v1

--- a/solution.py
+++ b/solution.py
@@ -21,16 +21,16 @@
 
 def kernel(
     n, cores, back, slots, chunk,
-    freq_ref, seg_ref, owners_hbm, rows_hbm, q_hbm, ak_hbm, av_hbm,
+    freq_ref, seg_hbm, owners_hbm, rows_hbm, q_hbm, ak_hbm, av_hbm,
     out_ref, kv_ref,
-    qv, ak, av, qf, acc, m_ref, l_ref, held, owners,
+    qv, ak, av, qf, acc, m_ref, l_ref, held, values, owners, seg_ref,
     local_sem, send_sem, recv_sem, fsend_sem, frecv_sem, osend_sem, orecv_sem,
 ):
     c = lax.axis_index("ctx")
     d = lax.axis_index("dec")
-    rows = rows_hbm.shape[0]
+    rows = rows_hbm.shape[1]
     heads = ak_hbm.shape[0]
-    part = rows // cores
+    part = (LATENT + ROPE) // cores
     scale = (NOPE + ROPE) ** (-0.5)
     last = n - 1
 
@@ -40,6 +40,7 @@
         pltpu.make_async_copy(ak_hbm, ak, local_sem.at[2]),
         pltpu.make_async_copy(av_hbm, av, local_sem.at[3]),
         pltpu.make_async_copy(owners_hbm, owners.at[last], local_sem.at[4]),
+        pltpu.make_async_copy(seg_hbm, seg_ref, local_sem.at[5]),
     ]
     for load in loads:
         load.start()
@@ -105,6 +106,7 @@
     sine = jnp.sin(angles)
     sine = jnp.where(low, -sine, sine)
 
+    loads[5].wait()
     seg_now = seg_ref[pl.ds(c, 1), :].astype(jnp.float32)
     query_seg = jnp.transpose(jnp.broadcast_to(seg_now, (rows, rows)))
     row_id = lax.broadcasted_iota(jnp.int32, (rows, rows), 0)
@@ -149,11 +151,12 @@
 
     def scores_of(i, keys, mask):
         q = qf[pl.ds(i * chunk, chunk)].reshape(size, LATENT + ROPE)
-        s = lax.dot_general(
-            q, keys, (((1,), (1,)), ((), ())), preferred_element_type=jnp.float32
-        )
-        s = s.reshape(chunk, rows, keys.shape[0]) * scale
-        return jnp.where(mask[None], s, NEG).reshape(size, keys.shape[0])
+        s = jnp.dot(q, keys, preferred_element_type=jnp.float32)
+        s = s.reshape(chunk, rows, keys.shape[1]) * scale
+        return jnp.where(mask[None], s, NEG).reshape(size, keys.shape[1])
+
+    def spread(j, at):
+        values[at:at + rows] = jnp.transpose(held[last - j, :LATENT])
 
     def finish(i, total, sums):
         latent = (total / sums).astype(jnp.bfloat16)
@@ -162,6 +165,8 @@
             out_ref[:, pl.ds(pl.multiple_of(h * VDIM, VDIM), VDIM)] = jnp.dot(
                 latent[k * rows:(k + 1) * rows], av[h], preferred_element_type=jnp.float32
             ).astype(jnp.bfloat16)
+
+    spread(0, 0)
 
     @pl.loop(0, heads // chunk)
     def _(i):
@@ -173,7 +178,7 @@
         m_ref[at] = top
         l_ref[at] = jnp.sum(e, axis=1, keepdims=True)
         acc[at] = jnp.dot(
-            e.astype(jnp.bfloat16), keys[:, :LATENT], preferred_element_type=jnp.float32
+            e.astype(jnp.bfloat16), values[:rows], preferred_element_type=jnp.float32
         )
 
     groups = [list(range(j, min(j + 2, back + 1))) for j in range(1, back + 1, 2)]
@@ -192,11 +197,12 @@
         for j in group:
             settle(j)
         mask = jnp.concatenate([mask_of(j) for j in reversed(group)], axis=1)
-        lo, hi = last - group[-1], last - group[0] + 1
+        for at, j in enumerate(reversed(group)):
+            spread(j, at * rows)
         final = g == len(groups) - 1
 
         def step(i):
-            keys = held[lo:hi].reshape((hi - lo) * rows, LATENT + ROPE)
+            keys = jnp.concatenate([held[last - j] for j in reversed(group)], axis=1)
             s = scores_of(i, keys, mask)
             at = pl.ds(pl.multiple_of(i * size, size), size)
             before = m_ref[at]
@@ -205,7 +211,8 @@
             shrink = jnp.exp(before - top)
             sums = l_ref[at] * shrink + jnp.sum(e, axis=1, keepdims=True)
             total = acc[at] * shrink + jnp.dot(
-                e.astype(jnp.bfloat16), keys[:, :LATENT], preferred_element_type=jnp.float32
+                e.astype(jnp.bfloat16), values[:len(group) * rows],
+                preferred_element_type=jnp.float32,
             )
             if final:
                 finish(i, total, sums)
@@ -232,14 +239,14 @@
     before_tri = (row_id < col_id).astype(jnp.bfloat16)
     slot_id = lax.broadcasted_iota(jnp.int32, (slots, rows), 0).astype(jnp.float32)
     for j in range(n):
-        named = owners[last - j, 0:8] == me
+        named = jnp.broadcast_to(owners[last - j], (8, rows)) == me
         rank = jnp.dot(
             named.astype(jnp.bfloat16), before_tri, preferred_element_type=jnp.float32
         )
         rank = jnp.where(named, rank, -1.0)
         picker = (jnp.broadcast_to(rank[0:1], (slots, rows)) == slot_id).astype(jnp.bfloat16)
-        kv_ref[0, lax.rem(c - j + n, n)] = jnp.dot(
-            picker, held[last - j], preferred_element_type=jnp.float32
+        kv_ref[0, lax.rem(c - j + n, n)] = lax.dot_general(
+            picker, held[last - j], (((1,), (1,)), ((), ())), preferred_element_type=jnp.float32
         ).astype(jnp.bfloat16)
 
     for j in range(1, n):
@@ -260,9 +267,9 @@
     frequency = 10000.0 ** (-jnp.arange(ROPE // 2, dtype=jnp.float32) * 2.0 / ROPE)
     frequency = jnp.broadcast_to(jnp.tile(frequency, 4)[None, :], (8, 2 * ROPE))
     segment_rows = segments.reshape(n, rows)
-    owner_rows = jnp.broadcast_to(owners.reshape(1, rows), (8, rows))
+    owner_rows = owners.reshape(1, rows)
     vmem = pl.BlockSpec(memory_space=pltpu.VMEM)
-    hbm = pl.BlockSpec(memory_space=pl.ANY)
+    hbm = pl.BlockSpec(memory_space=pltpu.HBM)
     dma = pltpu.SemaphoreType.DMA
     return tuple(pl.pallas_call(
         functools.partial(kernel, n, cores, back, slots, chunk),
@@ -270,7 +277,7 @@
             jax.ShapeDtypeStruct((rows, heads * VDIM), jnp.bfloat16),
             jax.ShapeDtypeStruct((1, n, slots, width), jnp.bfloat16),
         ),
-        in_specs=[vmem, vmem, hbm, hbm, hbm, hbm, hbm],
+        in_specs=[vmem, hbm, hbm, hbm, hbm, hbm, hbm],
         out_specs=(vmem, vmem),
         scratch_shapes=[
             pltpu.VMEM(queries.shape, jnp.bfloat16),
@@ -280,9 +287,11 @@
             pltpu.VMEM((heads * rows, LATENT), jnp.float32),
             pltpu.VMEM((heads * rows, 1), jnp.float32),
             pltpu.VMEM((heads * rows, 1), jnp.float32),
-            pltpu.VMEM((n, rows, width), jnp.bfloat16),
-            pltpu.VMEM((n, 8, rows), jnp.int32),
-            dma((5,)),
+            pltpu.VMEM((n, width, rows), jnp.bfloat16),
+            pltpu.VMEM((2 * rows, LATENT), jnp.bfloat16),
+            pltpu.VMEM((n, 1, rows), jnp.int32),
+            pltpu.VMEM((n, rows), jnp.int32),
+            dma((6,)),
             dma((n,)),
             dma((n,)),
             dma((n, cores)),
@@ -291,9 +300,9 @@
             dma((n,)),
         ],
         compiler_params=pltpu.CompilerParams(
-            collective_id=0, has_side_effects=True, vmem_limit_bytes=48 * 1024 * 1024
+            collective_id=0, has_side_effects=True, vmem_limit_bytes=66200000
         ),
-    )(frequency, segment_rows, owner_rows, latent_rows, queries, absorb_key, absorb_value))
+    )(frequency, segment_rows, owner_rows, latent_rows.T, queries, absorb_key, absorb_value))
 
 
 def solution(mesh):

time: 32.2 us -> 27.5 us (0.85)
  the two profiles are of different devices: /device:TPU:21 before, /device:TPU:1 now
where the time goes in v2:
time: 27.5 us; the launch traced here: 27.3 us
  Pallas kernels  22.5 us (82%)
  local copies, waits for them, and re-layouts  4.16 us (15%)
  between operations  0.65 us (2%)
    pallas_call x1, Pallas kernels, on_device(): pl.pallas_call(functools.partial(kernel, n, cores, back, slots, chunk), o...  22.5 us
    unnamed x2, local copies, waits for them, and re-layouts  3.48 us
    broadcast_in_dim x2, local copies, waits for them, and re-layouts, on_device(): frequency = jnp.broadcast_to(jnp.tile(frequency, 4)[None, :], (8, 2 * ROPE))  0.68 us

profile of v2, /device:TPU:1, one launch (start us, length us, event | category | flops | bytes accessed | tf_op | source)
XLA Modules:
  0.0 27.3 jit_solution(15756059349281464621)
XLA Ops:
  0.7 0.1 broadcast_in_dim.7
  0.7 0.6 %broadcast_in_dim.8.freq_ref = f32[8,128]{1,0:T(8,128)} broadcast(f32[128]{0:T(128)S(1)} %broadcast_in_dim.7), dimensions={1} | broadcast | bytes 4608 | tf_op jit(solution)/shard_map/broadcast_in_dim | solution.py:268
  1.3 22.5 %shard_map.77 = (bf16[128,2048]{1,0:T(8,128)(2,1)}, bf16[1,4,32,576]{3,2,1,0:T(8,128)(2,1)}) custom-call(f32[8,128]{1,0:T(8,128)} %broadcast_in_dim.8.freq_ref, s32[4,128]{1,0:T(4,128)} %bitcast.4, s32[1,128]{1,0:T(1,128)} %bitcast.5, bf16[576,128]{1,0:T(8,128)(2,1)} %bitcast.3, bf16[128,3072]{1,0:T(8,128)(2,1)} %q_hbm.1, bf16[16,128,512]{2,1,0:T(8,128)(2,1)} %ak_hbm.1, ...), custom_call_target="tpu_custom_call" | custom-call | tf_op jit(solution)/shard_map/pallas_call | solution.py:274
  23.8 1.9 %copy.10 = bf16[128,2048]{1,0:T(8,128)(2,1)} copy(bf16[128,2048]{1,0:T(8,128)(2,1)} %get-tuple-element.4) | data formatting | bytes 1048576
  25.7 1.6 %copy.11 = bf16[1,4,32,576]{3,2,1,0:T(8,128)(2,1)} copy(bf16[1,4,32,576]{3,2,1,0:T(8,128)(2,1)} %get-tuple-element.5) | data formatting | bytes 294912
  (2 shorter events, 0.0 us)

commit v3 on v2

--- a/solution.py
+++ b/solution.py
@@ -2,6 +2,7 @@
 
 import jax
 import jax.numpy as jnp
+import numpy as np
 from jax import lax
 from jax.experimental import pallas as pl
 from jax.experimental.pallas import tpu as pltpu
@@ -23,8 +24,9 @@
     n, cores, back, slots, chunk,
     freq_ref, seg_hbm, owners_hbm, rows_hbm, q_hbm, ak_hbm, av_hbm,
     out_ref, kv_ref,
-    qv, ak, av, qf, acc, m_ref, l_ref, held, values, owners, seg_ref,
+    qv, ak, av, qf, acc, m_ref, l_ref, held, values, owners, seg_ref, compact,
     local_sem, send_sem, recv_sem, fsend_sem, frecv_sem, osend_sem, orecv_sem,
+    ksend_sem, krecv_sem,
 ):
     c = lax.axis_index("ctx")
     d = lax.axis_index("dec")
@@ -57,9 +59,19 @@
     pl.semaphore_wait(barrier, n - 1 + cores - 1)
 
     mine = pl.ds(pl.multiple_of(d * part, part), part)
-    sends = {}
+    sends, osends, ksends = {}, {}, {}
     for j in range(1, n):
         target = {"ctx": lax.rem(c + j, n)}
+        ksends[j] = pltpu.make_async_remote_copy(
+            src_ref=compact.at[j],
+            dst_ref=kv_ref.at[0, c],
+            send_sem=ksend_sem.at[j],
+            recv_sem=krecv_sem.at[j],
+            device_id=target,
+            device_id_type=MESH,
+        )
+        if j > back:
+            continue
         sends[j] = pltpu.make_async_remote_copy(
             src_ref=rows_hbm.at[mine],
             dst_ref=held.at[last - j, mine],
@@ -68,26 +80,32 @@
             device_id=target,
             device_id_type=MESH,
         )
-        sends[j].start()
-    osends = []
-    for j in range(1, n):
-        copy = pltpu.make_async_remote_copy(
+        osends[j] = pltpu.make_async_remote_copy(
             src_ref=owners_hbm,
             dst_ref=owners.at[last - j],
             send_sem=osend_sem.at[j],
             recv_sem=orecv_sem.at[j],
-            device_id={"ctx": lax.rem(c + j, n)},
+            device_id=target,
             device_id_type=MESH,
         )
-        copy.start()
-        osends.append(copy)
+
+    for j in sends:
+        @pl.when(c + j < n)
+        def _():
+            sends[j].start()
+    for j in sends:
+        @pl.when(c + j < n)
+        def _():
+            osends[j].start()
+
+        @pl.when(c < j)
+        def _():
+            held[last - j] = jnp.zeros_like(held[last - j])
 
     forwards = {}
-
-    def forward(j):
-        sends[j].wait_recv()
+    for j in sends:
         for k in range(1, cores):
-            copy = pltpu.make_async_remote_copy(
+            forwards[j, k] = pltpu.make_async_remote_copy(
                 src_ref=held.at[last - j, mine],
                 dst_ref=held.at[last - j, mine],
                 send_sem=fsend_sem.at[j, k],
@@ -95,8 +113,13 @@
                 device_id={"dec": lax.rem(d + k, cores)},
                 device_id_type=MESH,
             )
-            copy.start()
-            forwards[j, k] = copy
+
+    def forward(j):
+        @pl.when(c >= j)
+        def _():
+            sends[j].wait_recv()
+            for k in range(1, cores):
+                forwards[j, k].start()
 
     lane = lax.broadcasted_iota(jnp.int32, (rows, 2 * ROPE), 1) % ROPE
     position = (lax.broadcasted_iota(jnp.int32, (rows, 2 * ROPE), 0) + c * rows).astype(jnp.float32)
@@ -119,6 +142,30 @@
             return same & (col_id <= row_id)
         valid = jnp.broadcast_to(c, (rows, rows)) >= j
         return same & valid
+
+    loads[0].wait()
+    loads[4].wait()
+    before_tri = (row_id < col_id).astype(jnp.bfloat16)
+
+    def ranks(named):
+        rank = jnp.dot(
+            named.astype(jnp.bfloat16), before_tri, preferred_element_type=jnp.float32
+        )
+        return jnp.where(named, rank, -1.0)
+
+    def pick(picker, block):
+        return lax.dot_general(
+            picker.astype(jnp.bfloat16), block, (((1,), (1,)), ((), ())),
+            preferred_element_type=jnp.float32,
+        ).astype(jnp.bfloat16)
+
+    line = lax.broadcasted_iota(jnp.int32, (n * slots, rows), 0)
+    wanted = lax.rem(c + line // slots, n) * cores + d
+    named = jnp.broadcast_to(owners[last], (n * slots, rows)) == wanted
+    picked = pick(ranks(named) == (line % slots).astype(jnp.float32), held[last])
+    kv_ref[0, c] = picked[:slots]
+    for j in range(1, n):
+        compact[j] = picked[j * slots:(j + 1) * slots]
 
     loads[1].wait()
     loads[2].wait()
@@ -143,9 +190,15 @@
                 qp[:, start:start + NOPE], ak[2 * p + k], preferred_element_type=jnp.float32
             ).astype(jnp.bfloat16)
 
-    if n > 1:
+    for j in range(1, n):
+        if j > back:
+            ksends[j].start()
+        else:
+            @pl.when(c + j >= n)
+            def _():
+                ksends[j].start()
+    if back:
         forward(1)
-    loads[0].wait()
     size = chunk * rows
     own_mask = mask_of(0)
 
@@ -182,12 +235,12 @@
         )
 
     groups = [list(range(j, min(j + 2, back + 1))) for j in range(1, back + 1, 2)]
-    waited = set()
 
     def settle(j):
-        for k in range(1, cores):
-            forwards[j, k].wait_recv()
-        waited.add(j)
+        @pl.when(c >= j)
+        def _():
+            for k in range(1, cores):
+                forwards[j, k].wait_recv()
 
     loads[3].wait()
     for g, group in enumerate(groups):
@@ -221,38 +274,72 @@
                 l_ref[at] = sums
                 acc[at] = total
 
-        middle = (heads // chunk) // 2 if final else heads // chunk
-        pl.loop(0, middle)(step)
-        if final:
-            for j in range(back + 1, n):
-                forward(j)
-            pl.loop(middle, heads // chunk)(step)
-
+        pl.loop(0, heads // chunk)(step)
+
+    me = c * cores + d
+    slot_id = lax.broadcasted_iota(jnp.int32, (slots, rows), 0).astype(jnp.float32)
     for j in range(1, n):
-        if j not in waited:
-            settle(j)
-    loads[4].wait()
-    for copy in osends:
-        copy.wait()
-
-    me = c * cores + d
-    before_tri = (row_id < col_id).astype(jnp.bfloat16)
-    slot_id = lax.broadcasted_iota(jnp.int32, (slots, rows), 0).astype(jnp.float32)
-    for j in range(n):
-        named = jnp.broadcast_to(owners[last - j], (8, rows)) == me
-        rank = jnp.dot(
-            named.astype(jnp.bfloat16), before_tri, preferred_element_type=jnp.float32
-        )
-        rank = jnp.where(named, rank, -1.0)
-        picker = (jnp.broadcast_to(rank[0:1], (slots, rows)) == slot_id).astype(jnp.bfloat16)
-        kv_ref[0, lax.rem(c - j + n, n)] = lax.dot_general(
-            picker, held[last - j], (((1,), (1,)), ((), ())), preferred_element_type=jnp.float32
-        ).astype(jnp.bfloat16)
-
-    for j in range(1, n):
-        sends[j].wait_send()
-        for k in range(1, cores):
-            forwards[j, k].wait_send()
+        if j > back:
+            ksends[j].wait()
+            continue
+
+        @pl.when(c + j >= n)
+        def _():
+            ksends[j].wait_send()
+
+        @pl.when(c < j)
+        def _():
+            ksends[j].wait_recv()
+
+        @pl.when(c + j < n)
+        def _():
+            sends[j].wait_send()
+            osends[j].wait_send()
+
+        @pl.when(c >= j)
+        def _():
+            osends[j].wait_recv()
+            named = jnp.broadcast_to(owners[last - j], (8, rows)) == me
+            rank = jnp.broadcast_to(ranks(named)[0:1], (slots, rows))
+            kv_ref[0, c - j] = pick(rank == slot_id, held[last - j])
+            for k in range(1, cores):
+                forwards[j, k].wait_send()
+
+
+def passing(pieces, *refs):
+    count = len(refs) // 3
+    sources, targets, held, (sem,) = (
+        refs[:count], refs[count:2 * count], refs[2 * count:3 * count], refs[3 * count:]
+    )
+    loads, stores = [], []
+    for i, (source, target, room) in enumerate(zip(sources, targets, held)):
+        step = source.shape[0] // pieces[i]
+        for k in range(pieces[i]):
+            at = pl.ds(k * step, step)
+            spot = len(loads)
+            loads.append(pltpu.make_async_copy(source.at[at], room.at[at], sem.at[0, spot]))
+            stores.append(pltpu.make_async_copy(room.at[at], target.at[at], sem.at[1, spot]))
+    for load in loads:
+        load.start()
+    for load, store in zip(loads, stores):
+        load.wait()
+        store.start()
+    for store in stores:
+        store.wait()
+
+
+def hand_over(*arrays):
+    pieces = (4, 1)
+    hbm = pl.BlockSpec(memory_space=pltpu.HBM)
+    return pl.pallas_call(
+        functools.partial(passing, pieces),
+        out_shape=tuple(jax.ShapeDtypeStruct(a.shape, a.dtype) for a in arrays),
+        in_specs=[hbm] * len(arrays),
+        out_specs=(hbm,) * len(arrays),
+        scratch_shapes=[pltpu.VMEM(a.shape, a.dtype) for a in arrays]
+        + [pltpu.SemaphoreType.DMA((2, sum(pieces)))],
+        compiler_params=pltpu.CompilerParams(vmem_limit_bytes=66200000),
+    )(*arrays)
 
 
 def on_device(sizes, queries, latent_rows, segments, owners, absorb_key, absorb_value):
@@ -264,14 +351,14 @@
     back = min(n - 1, cdiv(tokens // 2 - 1, rows))
     slots = max(2, 2 * rows // (n * cores))
     chunk = 4
-    frequency = 10000.0 ** (-jnp.arange(ROPE // 2, dtype=jnp.float32) * 2.0 / ROPE)
-    frequency = jnp.broadcast_to(jnp.tile(frequency, 4)[None, :], (8, 2 * ROPE))
+    frequency = 10000.0 ** (-np.arange(ROPE // 2, dtype=np.float32) * 2.0 / ROPE)
+    frequency = np.tile(frequency.astype(np.float32), 4)[None, :]
     segment_rows = segments.reshape(n, rows)
     owner_rows = owners.reshape(1, rows)
     vmem = pl.BlockSpec(memory_space=pltpu.VMEM)
     hbm = pl.BlockSpec(memory_space=pltpu.HBM)
     dma = pltpu.SemaphoreType.DMA
-    return tuple(pl.pallas_call(
+    results = pl.pallas_call(
         functools.partial(kernel, n, cores, back, slots, chunk),
         out_shape=(
             jax.ShapeDtypeStruct((rows, heads * VDIM), jnp.bfloat16),
@@ -291,18 +378,22 @@
             pltpu.VMEM((2 * rows, LATENT), jnp.bfloat16),
             pltpu.VMEM((n, 1, rows), jnp.int32),
             pltpu.VMEM((n, rows), jnp.int32),
+            pltpu.VMEM((n, slots, width), jnp.bfloat16),
             dma((6,)),
             dma((n,)),
             dma((n,)),
             dma((n, cores)),
             dma((n, cores)),
+            dma((n,)),
+            dma((n,)),
             dma((n,)),
             dma((n,)),
         ],
         compiler_params=pltpu.CompilerParams(
             collective_id=0, has_side_effects=True, vmem_limit_bytes=66200000
         ),
-    )(frequency, segment_rows, owner_rows, latent_rows.T, queries, absorb_key, absorb_value))
+    )(frequency, segment_rows, owner_rows, latent_rows.T, queries, absorb_key, absorb_value)
+    return tuple(hand_over(*results))
 
 
 def solution(mesh):

time: 27.5 us -> 23.6 us (0.86)
  the two profiles are of different devices: /device:TPU:1 before, /device:TPU:21 now
where the time goes in v3:
time: 23.6 us; the launch traced here: 23.5 us
  Pallas kernels  22.8 us (97%)
  between operations  0.64 us (3%)
    pallas_call x1, Pallas kernels, on_device(): pl.pallas_call(functools.partial(kernel, n, cores, back, slots, chunk), o...  20.9 us
    pallas_call x1, Pallas kernels, hand_over(): pl.pallas_call(functools.partial(passing, pieces), out_shape=tuple((jax.S...  1.93 us

profile of v3, /device:TPU:21, one launch (start us, length us, event | category | flops | bytes accessed | tf_op | source)
XLA Modules:
  0.0 23.5 jit_solution(5112359058725423189)
XLA Ops:
  0.6 20.9 %shard_map.86 = (bf16[128,2048]{1,0:T(8,128)(2,1)}, bf16[1,4,32,576]{3,2,1,0:T(8,128)(2,1)}) custom-call(f32[1,128]{1,0:T(1,128)} %constant.2.clone.freq_ref, s32[4,128]{1,0:T(4,128)} %bitcast.4, s32[1,128]{1,0:T(1,128)} %bitcast.5, bf16[576,128]{1,0:T(8,128)(2,1)} %bitcast.3, bf16[128,3072]{1,0:T(8,128)(2,1)} %q_hbm.1, bf16[16,128,512]{2,1,0:T(8,128)(2,1)} %ak_hbm.1, ...), custom_call_target="tpu_custom_call" | custom-call | tf_op jit(solution)/shard_map/pallas_call | solution.py:361
  21.6 1.9 %shard_map.87 = (bf16[128,2048]{1,0:T(8,128)(2,1)}, bf16[1,4,32,576]{3,2,1,0:T(8,128)(2,1)}) custom-call(bf16[128,2048]{1,0:T(8,128)(2,1)} %get-tuple-element.4.refs_0_, bf16[1,4,32,576]{3,2,1,0:T(8,128)(2,1)} %get-tuple-element.5.refs_1_), custom_call_target="tpu_custom_call" | custom-call | tf_op jit(solution)/shard_map/pallas_call | solution.py:334

commit v4 on v3

--- a/solution.py
+++ b/solution.py
@@ -350,7 +350,7 @@
     tokens = segments.shape[0]
     back = min(n - 1, cdiv(tokens // 2 - 1, rows))
     slots = max(2, 2 * rows // (n * cores))
-    chunk = 4
+    chunk = heads
     frequency = 10000.0 ** (-np.arange(ROPE // 2, dtype=np.float32) * 2.0 / ROPE)
     frequency = np.tile(frequency.astype(np.float32), 4)[None, :]
     segment_rows = segments.reshape(n, rows)

time: 23.6 us -> 22.2 us (0.941)
  the two profiles are of different devices: /device:TPU:21 before, /device:TPU:31 now
where the time goes in v4:
time: 22.2 us; the launch traced here: 22 us
  Pallas kernels  21.4 us (96%)
  between operations  0.64 us (3%)
    pallas_call x1, Pallas kernels, on_device(): pl.pallas_call(functools.partial(kernel, n, cores, back, slots, chunk), o...  19.4 us
    pallas_call x1, Pallas kernels, hand_over(): pl.pallas_call(functools.partial(passing, pieces), out_shape=tuple((jax.S...  1.93 us

profile of v4, /device:TPU:31, one launch (start us, length us, event | category | flops | bytes accessed | tf_op | source)
XLA Modules:
  0.0 22.0 jit_solution(13579159923589097515)
XLA Ops:
  0.6 19.4 %shard_map.86 = (bf16[128,2048]{1,0:T(8,128)(2,1)}, bf16[1,4,32,576]{3,2,1,0:T(8,128)(2,1)}) custom-call(f32[1,128]{1,0:T(1,128)} %constant.2.clone.freq_ref, s32[4,128]{1,0:T(4,128)} %bitcast.4, s32[1,128]{1,0:T(1,128)} %bitcast.5, bf16[576,128]{1,0:T(8,128)(2,1)} %bitcast.3, bf16[128,3072]{1,0:T(8,128)(2,1)} %q_hbm.1, bf16[16,128,512]{2,1,0:T(8,128)(2,1)} %ak_hbm.1, ...), custom_call_target="tpu_custom_call" | custom-call | tf_op jit(solution)/shard_map/pallas_call | solution.py:361
  20.1 1.9 %shard_map.87 = (bf16[128,2048]{1,0:T(8,128)(2,1)}, bf16[1,4,32,576]{3,2,1,0:T(8,128)(2,1)}) custom-call(bf16[128,2048]{1,0:T(8,128)(2,1)} %get-tuple-element.4.refs_0_, bf16[1,4,32,576]{3,2,1,0:T(8,128)(2,1)} %get-tuple-element.5.refs_1_), custom_call_target="tpu_custom_call" | custom-call | tf_op jit(solution)/shard_map/pallas_call | solution.py:334

commit v5 on v4

--- a/solution.py
+++ b/solution.py
@@ -171,7 +171,7 @@
     loads[2].wait()
     pair_width = 2 * (NOPE + ROPE)
 
-    @pl.loop(0, heads // 2)
+    @pl.loop(0, heads // 2, unroll=2)
     def _(p):
         qp = qv[:, pl.ds(pl.multiple_of(p * pair_width, 128), pair_width)]
         rope = jnp.concatenate(

time: 22.2 us -> 22.2 us (level)
  the two profiles are of different devices: /device:TPU:31 before, /device:TPU:21 now
where the time goes in v5:
time: 22.2 us; the launch traced here: 21.9 us
  Pallas kernels  21.3 us (96%)
  between operations  0.64 us (3%)
    pallas_call x1, Pallas kernels, on_device(): pl.pallas_call(functools.partial(kernel, n, cores, back, slots, chunk), o...  19.3 us
    pallas_call x1, Pallas kernels, hand_over(): pl.pallas_call(functools.partial(passing, pieces), out_shape=tuple((jax.S...  1.93 us

profile of v5, /device:TPU:21, one launch (start us, length us, event | category | flops | bytes accessed | tf_op | source)
XLA Modules:
  0.0 21.9 jit_solution(5223564144838707943)
XLA Ops:
  0.6 19.3 %shard_map.86 = (bf16[128,2048]{1,0:T(8,128)(2,1)}, bf16[1,4,32,576]{3,2,1,0:T(8,128)(2,1)}) custom-call(f32[1,128]{1,0:T(1,128)} %constant.2.clone.freq_ref, s32[4,128]{1,0:T(4,128)} %bitcast.4, s32[1,128]{1,0:T(1,128)} %bitcast.5, bf16[576,128]{1,0:T(8,128)(2,1)} %bitcast.3, bf16[128,3072]{1,0:T(8,128)(2,1)} %q_hbm.1, bf16[16,128,512]{2,1,0:T(8,128)(2,1)} %ak_hbm.1, ...), custom_call_target="tpu_custom_call" | custom-call | tf_op jit(solution)/shard_map/pallas_call | solution.py:361
  20.0 1.9 %shard_map.87 = (bf16[128,2048]{1,0:T(8,128)(2,1)}, bf16[1,4,32,576]{3,2,1,0:T(8,128)(2,1)}) custom-call(bf16[128,2048]{1,0:T(8,128)(2,1)} %get-tuple-element.4.refs_0_, bf16[1,4,32,576]{3,2,1,0:T(8,128)(2,1)} %get-tuple-element.5.refs_1_), custom_call_target="tpu_custom_call" | custom-call | tf_op jit(solution)/shard_map/pallas_call | solution.py:334
